TPU v7x, 1024 devices: a whole 4x8x16 slice. The times are simulated.
1024 devices in a mesh: section: 16 (over x, y_hi), dp: 4 (over y_lo, core), tensor: 16 (over z).
Axes of the slice: x: 4, y: 8 (y_hi: 4, y_lo: 2; y = y_hi * 2 + y_lo), z: 16, core: 2. Of those that a mesh axis runs over, the one named last changes fastest.
Arguments:
- queries: bfloat16 [8192, 8192], P(('section', 'dp'), 'tensor'), may hold values from -6 to 6
- images: bfloat16 [4, 3200, 8192], P('dp', 'section', 'tensor'), may hold values from -6 to 6
- kv_weight: bfloat16 [2, 8192, 1024], P(None, 'tensor', 'dp'), may hold values from -0.0625 to 0.0625
- q_gain: float32 [128], replicated, may hold values from 1 to 10
- k_gain: float32 [128], replicated, may hold values from 0.1 to 1.9
- tile_mask: int32 [8192, 4], P(('section', 'dp')), may hold values 0 or 1
Outputs:
- context: bfloat16 [8192, 8192], P(('section', 'dp'), 'tensor')
All inputs are finite; a program needn't handle non-finite values. No bound on the sum of `tile_mask` on one device may be relied on, other than what follows from the above.
Results may differ from a plain program's by a relative error of at most 0.04.
Values may be sent and summed in bfloat16 or wider, within the bound.
A program may use at most 32 MiB of HBM per device.

v0:
```python
import jax
import jax.numpy as jnp
from jax import lax
from jax.sharding import PartitionSpec as P

EPSILON = 1e-05
MASKED_SCORE = -1e30


def copy_for_each(shard, axis):
    size = lax.axis_size(axis)
    return lax.all_to_all(
        jnp.broadcast_to(shard[None], (size, *shard.shape)), axis, 0, 0, tiled=True
    )


def in_order(parts, dim):
    parts = jnp.moveaxis(parts, 0, dim)
    dims = parts.shape
    return parts.reshape(*dims[:dim], dims[dim] * dims[dim + 1], *dims[dim + 2 :])


def gather_directly(shard, axis, dim):
    parts = copy_for_each(shard, axis)
    return in_order(parts, dim)


def cut_along(shard, dim, size):
    dims = shard.shape
    parts = shard.reshape(*dims[:dim], size, dims[dim] // size, *dims[dim + 1 :])
    return jnp.moveaxis(parts, dim, 0)


def summed_on_arrival(shard, axis, dim):
    size = lax.axis_size(axis)
    parts = lax.all_to_all(cut_along(shard, dim, size), axis, 0, 0, tiled=True)
    return jnp.sum(parts.astype(jnp.float32), axis=0)


def partner_2(shard, axis, stride):
    return lax.ppermute(shard, axis, [(i, i ^ 1 << stride) for i in range(lax.axis_size(axis))])


def in_one_piece(arrays, axis, dim, along):
    ends, at = ([], 0)
    for a in arrays[:-1]:
        at += a.shape[along]
        ends.append(at)
    both = jnp.concatenate(arrays, axis=along)
    return tuple(jnp.split(lax.all_gather(both, axis, axis=dim, tiled=True), ends, axis=along))


def normalize(values, gain_vec):
    mean_sq = jnp.mean(values * values, axis=-1, keepdims=True)
    return values * lax.rsqrt(mean_sq + EPSILON) * gain_vec


def on_device(queries, images, kv_weight, q_gain, k_gain, tile_mask):
    n_section = lax.axis_size("section")
    head_dim = q_gain.shape[0]
    token_count = queries.shape[0]
    head_count = queries.shape[1] // head_dim
    tile_count = tile_mask.shape[1]
    image_rows = images.shape[1]
    features = images[0]
    weight_full = gather_directly(kv_weight, "dp", 2)
    half_dim = head_dim // 2
    groups = jnp.arange(1 * lax.axis_size("tensor"), dtype=jnp.int32)
    key_part = jnp.dot(features, weight_full[0], preferred_element_type=jnp.float32)
    value_part = jnp.dot(features, weight_full[1], preferred_element_type=jnp.float32)
    key_units = jnp.transpose(key_part.reshape(image_rows, -1, half_dim), (1, 0, 2))
    value_units = jnp.transpose(value_part.reshape(image_rows, -1, half_dim), (1, 0, 2))
    joined = jnp.concatenate([key_units, value_units], axis=2)
    own_half = summed_on_arrival(
        jnp.take(joined, groups, axis=0).astype(jnp.bfloat16), "tensor", 0
    )[0]
    partner = partner_2(own_half.astype(jnp.bfloat16), "tensor", 0).astype(own_half.dtype)
    is_odd = lax.axis_index("tensor") % 2 == 1
    lower_half = jnp.where(is_odd, partner, own_half)
    upper_half = jnp.where(is_odd, own_half, partner)
    key_raw = jnp.concatenate([lower_half[:, :half_dim], upper_half[:, :half_dim]], axis=1)
    value_raw = jnp.concatenate([lower_half[:, half_dim:], upper_half[:, half_dim:]], axis=1)
    key_rows = normalize(key_raw, k_gain).astype(jnp.bfloat16)
    value_rows = value_raw.astype(jnp.bfloat16)
    tile_len = image_rows * n_section // tile_count
    query_rows = queries.reshape(token_count, head_count, head_dim).astype(jnp.float32)
    q_normed = (normalize(query_rows, q_gain) * head_dim ** (-0.5)).astype(jnp.bfloat16)
    mask_float = tile_mask.astype(jnp.float32)
    row_max = jnp.full((head_count, token_count), MASKED_SCORE, jnp.float32)
    key_piece, value_piece = in_one_piece((key_rows, value_rows), "section", 0, 1)
    length = key_piece.shape[0]
    tiles_of = jnp.arange(length, dtype=jnp.int32) // tile_len
    onehot = (tiles_of[:, None] == jnp.arange(tile_count, dtype=jnp.int32)[None, :]).astype(
        jnp.float32
    )
    hidden_bias = jnp.where(jnp.dot(mask_float, onehot.T) > 0.5, 0.0, MASKED_SCORE)
    scores = (
        jnp.einsum("thd,nd->htn", q_normed, key_piece, preferred_element_type=jnp.float32)
        + hidden_bias[None]
    )
    new_max = jnp.maximum(row_max, jnp.max(scores, axis=2))
    weights = jnp.exp(scores - new_max[:, :, None])
    row_sum = jnp.sum(weights, axis=2)
    added = jnp.einsum(
        "htn,nd->htd", weights.astype(jnp.bfloat16), value_piece, preferred_element_type=jnp.float32
    )
    accumulated = added
    row_max, row_sum, accumulated = (new_max, row_sum, accumulated)
    has_any = jnp.sum(mask_float, axis=1) > 0.5
    divided = accumulated / jnp.where(has_any[None, :], row_sum, 1.0)[:, :, None]
    context = jnp.where(has_any[None, :, None], divided, 0.0)
    return (
        jnp.transpose(context, (1, 0, 2))
        .reshape(token_count, head_count * head_dim)
        .astype(jnp.bfloat16)
    )


def solution(mesh):
    in_specs = (
        P(("section", "dp"), "tensor"),
        P("dp", "section", "tensor"),
        P(None, "tensor", "dp"),
        P(),
        P(),
        P(("section", "dp"), None),
    )
    out_specs = P(("section", "dp"), "tensor")
    return jax.shard_map(
        on_device, mesh=mesh, in_specs=in_specs, out_specs=out_specs, check_vma=False
    )
```

profile of v0, /device:TPU:6, one launch (start us, length us, event | category | flops | bytes accessed | tf_op | source)
XLA Modules:
  0.0 189.4 jit_solution(159498103570190172)
XLA Ops:
  6.5 1.3 copy.43
  7.8 1.5 broadcast_in_dim.64
  9.4 3.6 %all-to-all-start = ((bf16[4,2,512,256]{2,3,1,0:T(8,128)(2,1)}), bf16[4,2,512,256]{2,3,1,0:T(8,128)(2,1)S(1)}, u32[]{:S(2)}, u32[]{:S(2)}) async-start(bf16[4,2,512,256]{2,3,1,0:T(8,128)(2,1)} %broadcast_in_dim.64), calls=%async_computation | async-start | bytes 4194304 | tf_op jit(solution)/shard_map/all_to_all | solution.py:12
  13.1 25.5 %all-to-all-done = bf16[4,2,512,256]{2,3,1,0:T(8,128)(2,1)S(1)} async-done(((bf16[4,2,512,256]{2,3,1,0:T(8,128)(2,1)}), bf16[4,2,512,256]{2,3,1,0:T(8,128)(2,1)S(1)}, u32[]{:S(2)}, u32[]{:S(2)}) %all-to-all-start) | async-done | bytes 2097184 | tf_op jit(solution)/shard_map/all_to_all | solution.py:12
  38.6 0.2 fusion.28
  38.9 0.5 convolution_bitcast_fusion
  39.3 0.5 convolution_bitcast_fusion.1
  39.8 0.2 pad_maximum_fusion
  40.0 0.6 copy.44
  40.6 0.7 gather_fusion
  41.3 0.2 fusion.7
  41.6 60.9 %all_to_all.10 = bf16[16,1,200,128]{3,2,1,0:T(8,128)(2,1)S(1)} all-to-all(bf16[16,1,200,128]{3,2,1,0:T(8,128)(2,1)S(1)} %fusion.7), channel_id=1, replica_groups=mesh['section'=16,'dp'=4,'tensor'=16] {'tensor'}, dimensions={0} | all-to-all | bytes 1638400 | tf_op jit(solution)/shard_map/all_to_all | solution.py:36
  102.6 3.2 %collective-permute-start = (bf16[200,128]{1,0:T(8,128)(2,1)S(1)}, bf16[200,128]{1,0:T(8,128)(2,1)S(1)}, u32[]{:S(2)}, u32[]{:S(2)}) collective-permute-start(bf16[200,128]{1,0:T(8,128)(2,1)S(1)} %convert_element_type.48), channel_id=1, source_target_pairs={{0,1},{1,0},{2,3},{3,2},{4,5},{5,4},{6,7},{7,6},{8,9},{9,8},{10,11... | collective-permute-start | bytes 153608 | tf_op jit(solution)/shard_map/ppermute | solution.py:41
  105.8 2.8 %collective-permute-done = bf16[200,128]{1,0:T(8,128)(2,1)S(1)} collective-permute-done((bf16[200,128]{1,0:T(8,128)(2,1)S(1)}, bf16[200,128]{1,0:T(8,128)(2,1)S(1)}, u32[]{:S(2)}, u32[]{:S(2)}) %collective-permute-start) | collective-permute-done | bytes 51232 | tf_op jit(solution)/shard_map/ppermute | solution.py:41
  109.2 0.7 pad_maximum_fusion.2
  110.1 0.2 multiply_reduce_fusion
  110.4 0.2 multiply_convert_fusion
  110.6 0.6 fusion.3
  111.2 65.9 %all-gather.2.cloned.1.call-done = bf16[3200,256]{1,0:T(8,128)(2,1)} async-done(((bf16[200,256]{1,0:T(8,128)(2,1)}), bf16[3200,256]{1,0:T(8,128)(2,1)}) %all-gather.2.cloned.1.call-update) | async-done | bytes 1638416 | tf_op jit(solution)/shard_map/all_gather | solution.py:50
  177.1 2.2 %fusion.29 = (f32[4,128]{1,0:T(4,128)S(1)}, f32[4,128,3200]{1,2,0:T(8,128)S(1)}) fusion(f32[128,3200]{0,1:T(8,128)S(1)} %fusion.3, bf16[128,4,128]{2,1,0:T(4,128)(2,1)S(1)} %multiply_convert_fusion, bf16[3200,256]{1,0:T(8,128)(2,1)} %all-gather.2.cloned.1.call-done), kind=kOutput, calls=%fused_computation.54 | convolution fusion | flops 422706688 | bytes 9144320 | tf_op jit(solution)/shard_map/thd,nd->htn/dot_general | solution.py:98
  179.2 0.9 fusion
  180.1 0.5 copy-done.1
  180.7 1.1 fusion.17
  181.7 0.8 copy.54
  (31 shorter events, 0.9 us)
Async XLA Ops:
  6.5 32.3 %copy-start = (bf16[1,200,512]{2,1,0:T(8,128)(2,1)S(1)}, bf16[1,200,512]{2,1,0:T(8,128)(2,1)}, u32[]{:S(2)}) copy-start(bf16[1,200,512]{2,1,0:T(8,128)(2,1)} %param.7) | copy-start | bytes 614404
  9.4 29.2 %all-to-all-start = ((bf16[4,2,512,256]{2,3,1,0:T(8,128)(2,1)}), bf16[4,2,512,256]{2,3,1,0:T(8,128)(2,1)S(1)}, u32[]{:S(2)}, u32[]{:S(2)}) async-start(bf16[4,2,512,256]{2,3,1,0:T(8,128)(2,1)} %broadcast_in_dim.64), calls=%async_computation | async-start | bytes 4194304 | tf_op jit(solution)/shard_map/all_to_all | solution.py:12
  13.0 164.1 %all-gather.2.cloned.1.call-start = ((), (), s32[]{:S(2)}) async-start(), calls=%async_computation.2 | async-start | bytes 1740800 | tf_op jit(solution)/shard_map/all_gather | solution.py:50
  41.6 67.5 %copy-start.4 = (f32[128]{0:T(128)S(1)}, f32[128]{0:T(128)}, u32[]{:S(2)}) copy-start(f32[128]{0:T(128)} %param.10) | copy-start | bytes 1540
  41.6 68.4 %copy-start.2 = (bf16[128,512]{1,0:T(8,128)(2,1)S(1)}, bf16[128,512]{1,0:T(8,128)(2,1)}, u32[]{:S(2)}) copy-start(bf16[128,512]{1,0:T(8,128)(2,1)} %param.6) | copy-start | bytes 393220
  41.6 68.5 %copy-start.3 = (s32[128,4]{0,1:T(4,128)S(1)}, s32[128,4]{0,1:T(4,128)}, u32[]{:S(2)}) copy-start(s32[128,4]{0,1:T(4,128)} %param.11) | copy-start | bytes 6148
  102.5 7.8 %copy-start.5 = (f32[128]{0:T(128)S(1)}, f32[128]{0:T(128)}, u32[]{:S(2)}) copy-start(f32[128]{0:T(128)} %param.9) | copy-start | bytes 1540
  102.6 6.0 %collective-permute-start = (bf16[200,128]{1,0:T(8,128)(2,1)S(1)}, bf16[200,128]{1,0:T(8,128)(2,1)S(1)}, u32[]{:S(2)}, u32[]{:S(2)}) collective-permute-start(bf16[200,128]{1,0:T(8,128)(2,1)S(1)} %convert_element_type.48), channel_id=1, source_target_pairs={{0,1},{1,0},{2,3},{3,2},{4,5},{5,4},{6,7},{7,6},{8,9},{9,8},{10,11... | collective-permute-start | bytes 153608 | tf_op jit(solution)/shard_map/ppermute | solution.py:41
  179.2 1.4 copy-start.1
Sparse Core Ops, SparseCore 0:
  110.1 66.9 all-gather.1
where the time goes:
time: 190 us; the launch traced here: 189 us
  waiting for transfers between devices  94.2 us (50%)
  blocking collectives  60.9 us (32%)
  between operations  13.7 us (7%)
  starting transfers between devices  6.82 us (4%)
  local copies, waits for them, and re-layouts  5.96 us (3%)
  matrix products  4.77 us (3%)
  other arithmetic  2.97 us (2%)
    all_gather x1, waiting for transfers between devices, in_one_piece(): lax.all_gather(both, axis, axis=dim, tiled=True)  65.9 us
    all_to_all x1, blocking collectives, summed_on_arrival(): parts = lax.all_to_all(cut_along(shard, dim, size), axis, 0, 0, tiled=True)  60.9 us
    all_to_all x1, waiting for transfers between devices, copy_for_each(): lax.all_to_all(jnp.broadcast_to(shard[None], (size, *shard.shape)), axis,...  25.5 us
  transfers between devices with their start and end apart: 3, of which 3 were waited for; matrix products, arithmetic and copies ran while one was open for 1% of the time, Pallas kernels for 0%

commit v1 on v0

v1 whole, which is shorter than its diff:
```python
import functools

import jax
import jax.numpy as jnp
from jax import lax
from jax.experimental import pallas as pl
from jax.experimental.pallas import tpu as pltpu
from jax.sharding import PartitionSpec as P

EPSILON = 1e-05
MASKED_SCORE = -1e30
MESH = pl.DeviceIdType.MESH
HD = 128
SPLIT = 96
UNIT = 104


def kernel(
    dims,
    img_hbm, w_hbm, q_hbm, qg_ref, kg_ref, mask_ref,
    out_ref,
    img, wbuf, qbuf, qs, bias, part, rp, rm, kv, scores, acc, top, total,
    load_sem, w_send, w_recv, p_send, p_recv, m_send, m_recv,
    kv_recv, z_send, y_relay, col_y, col_x, x_relay,
):
    n_x, n_y, n_t, heads = dims
    half_ring = n_t // 2
    s, d, t = lax.axis_index("section"), lax.axis_index("dp"), lax.axis_index("tensor")
    x, yh = s // n_y, s % n_y
    yl, core = d // 2, d % 2
    par = t % 2

    def section(a, b):
        return lax.rem(a + n_x, n_x) * n_y + lax.rem(b + n_y, n_y)

    partner = {"dp": d + 1 - 2 * core}
    y_next = {"section": section(x, yh + yl), "dp": (1 - yl) * 2 + core}
    y_prev = {"section": section(x, yh + yl - 1), "dp": (1 - yl) * 2 + core}
    z_next, z_prev = {"tensor": lax.rem(t + 1, n_t)}, {"tensor": lax.rem(t + n_t - 1, n_t)}
    z_pair = {"tensor": t + 1 - 2 * par}
    yh_next, yh_prev = {"section": section(x, yh + 1)}, {"section": section(x, yh - 1)}
    x_next, x_prev = {"section": section(x + 1, yh)}, {"section": section(x - 1, yh)}

    def remote(src, dst, send, recv, where):
        return pltpu.make_async_remote_copy(
            src_ref=src, dst_ref=dst, send_sem=send, recv_sem=recv, device_id=where, device_id_type=MESH
        )

    load_w = pltpu.make_async_copy(w_hbm, wbuf.at[d], load_sem.at[0])
    load_i = pltpu.make_async_copy(img_hbm.at[0], img, load_sem.at[1])
    load_q = pltpu.make_async_copy(q_hbm, qbuf, load_sem.at[2])
    load_w.start()
    load_i.start()
    load_q.start()

    barrier = pltpu.get_barrier_semaphore()
    near = (partner, y_next, y_prev, z_next, z_prev, yh_next, yh_prev, x_next, x_prev)
    for where in near:
        pl.semaphore_signal(barrier, inc=1, device_id=where, device_id_type=MESH)
    pl.semaphore_wait(barrier, len(near))

    other, far = d + 1 - 2 * core, (1 - yl) * 2 + core
    across = (1 - yl) * 2 + 1 - core
    w_far_k = remote(w_hbm.at[0], wbuf.at[d, 0], w_send.at[0], w_recv.at[0], y_next)
    w_far_v = remote(w_hbm.at[1], wbuf.at[d, 1], w_send.at[1], w_recv.at[1], y_prev)
    w_own = remote(w_hbm, wbuf.at[d], w_send.at[2], w_recv.at[2], partner)
    w_far_k.start()
    w_far_v.start()
    w_own.start()

    load_i.wait()
    load_w.wait()
    features = img[...]

    def project(group):
        for j in range(2):
            both = jnp.dot(features, wbuf[group, j], preferred_element_type=jnp.float32).astype(jnp.bfloat16)
            part[2 * group, j] = both[:, :HD]
            part[2 * group + 1, j] = both[:, HD:]

    project(d)

    load_q.wait()
    for h in range(heads):
        rows = qbuf[:, h * HD : (h + 1) * HD].astype(jnp.float32)
        mean_sq = jnp.mean(rows * rows, axis=-1, keepdims=True)
        normed = rows * lax.rsqrt(mean_sq + EPSILON) * qg_ref[...] * HD ** (-0.5)
        qs[h * HD : (h + 1) * HD, :] = normed.astype(jnp.bfloat16)
    tokens = mask_ref.shape[0]
    eye = (
        lax.broadcasted_iota(jnp.int32, (tokens, tokens), 0) == lax.broadcasted_iota(jnp.int32, (tokens, tokens), 1)
    ).astype(jnp.float32)
    seen = lax.dot_general(
        mask_ref[...].astype(jnp.float32), eye, (((0,), (0,)), ((), ())), preferred_element_type=jnp.float32
    )
    hidden = jnp.where(seen > 0.5, 0.0, MASKED_SCORE)
    for h in range(heads):
        bias[0:n_x, h * HD : (h + 1) * HD] = hidden
    top[...] = jnp.full_like(top, MASKED_SCORE)
    total[...] = jnp.zeros_like(total)
    acc[...] = jnp.zeros_like(acc)

    remote(w_hbm, wbuf.at[other], w_send.at[2], w_recv.at[2], partner).wait_recv()
    project(other)
    fwd = []
    for j in range(2):
        remote(w_hbm.at[j], wbuf.at[far, j], w_send.at[j], w_recv.at[j], partner).wait_recv()
        copy = remote(wbuf.at[far, j], wbuf.at[far, j], w_send.at[3 + j], w_recv.at[3 + j], partner)
        copy.start()
        fwd.append(copy)
    project(far)
    for j in range(2):
        remote(wbuf.at[far, j], wbuf.at[across, j], w_send.at[3 + j], w_recv.at[3 + j], partner).wait_recv()
    project(across)

    def own_part(u, j):
        start = pl.multiple_of(lax.rem(u, 2) * SPLIT, 16)
        return part.at[lax.div(u, 2), j, pl.ds(start, UNIT), :]

    sent = []
    for k in range(half_ring):
        for j in range(2):
            u = lax.rem(t + half_ring - k, n_t)
            if k == 0:
                src = own_part(u, j)
            else:
                src = rp.at[k - 1, j]
                remote(src, src, p_send.at[k - 1, j], p_recv.at[k - 1, j], z_next).wait_recv()
                src[...] = (src[...].astype(jnp.float32) + own_part(u, j)[...].astype(jnp.float32)).astype(jnp.bfloat16)
            copy = remote(src, rp.at[k, j], p_send.at[k, j], p_recv.at[k, j], z_next)
            copy.start()
            sent.append(copy)
            if k < half_ring - 1:
                u = lax.rem(t + half_ring + 1 + k, n_t)
                if k == 0:
                    src = own_part(u, j)
                else:
                    src = rm.at[k - 1, j]
                    remote(src, src, m_send.at[k - 1, j], m_recv.at[k - 1, j], z_prev).wait_recv()
                    src[...] = (src[...].astype(jnp.float32) + own_part(u, j)[...].astype(jnp.float32)).astype(
                        jnp.bfloat16
                    )
                copy = remote(src, rm.at[k, j], m_send.at[k, j], m_recv.at[k, j], z_prev)
                copy.start()
                sent.append(copy)

    for j in range(2):
        last_p, last_m = rp.at[half_ring - 1, j], rm.at[half_ring - 2, j]
        remote(last_m, last_m, m_send.at[half_ring - 2, j], m_recv.at[half_ring - 2, j], z_prev).wait_recv()
        remote(last_p, last_p, p_send.at[half_ring - 1, j], p_recv.at[half_ring - 1, j], z_next).wait_recv()
        rows = (
            own_part(t, j)[...].astype(jnp.float32)
            + last_p[...].astype(jnp.float32)
            + last_m[...].astype(jnp.float32)
        )
        if j == 0:
            mean_sq = jnp.mean(rows * rows, axis=-1, keepdims=True)
            rows = rows * lax.rsqrt(mean_sq + EPSILON) * kg_ref[...]
        kv[x, yh, par, j] = rows.astype(jnp.bfloat16)

    def place(a, b):
        return lax.rem(a + n_x, n_x), lax.rem(b + n_y, n_y)

    def chunk(a, b, q, send, where):
        a, b = place(a, b)
        return remote(kv.at[a, b, q], kv.at[a, b, q], send, kv_recv.at[a, b, q], where)

    def arrived(a, b, q):
        chunk(a, b, q, z_send, z_pair).wait_recv()

    def send_column(slot, b, q, i):
        for direction, where in enumerate((x_next, x_prev)):
            chunk(x, b, q, col_x.at[slot, i, direction], where).start()

    chunk(x, yh, par, z_send, z_pair).start()
    for i, q in enumerate((par, 1 - par)):
        if i == 1:
            arrived(x, yh, q)
        chunk(x, yh, q, col_y.at[i, 0], yh_next).start()
        chunk(x, yh, q, col_y.at[i, 1], yh_prev).start()
        send_column(0, yh, q, i)
    for i, q in enumerate((par, 1 - par)):
        arrived(x, yh - 1, q)

        @pl.when(q == 0)
        def _():
            chunk(x, yh - 1, 0, y_relay.at[0], yh_next).start()

        send_column(1, yh - 1, q, i)
        arrived(x, yh + 1, q)

        @pl.when(q == 1)
        def _():
            chunk(x, yh + 1, 1, y_relay.at[1], yh_prev).start()

        send_column(2, yh + 1, q, i)
    for q in range(2):
        arrived(x, yh + 2, q)
        send_column(3, yh + 2, q, q)

    def offset(n):
        return jnp.where(n == 0, 0, jnp.where(n == 1, 3, n - 1))

    def attend(i, carry):
        inner = (i >= 2) & (i < 6)
        own = i < 2
        base = jnp.where(own, 2 * i, 2 * (i - 6))
        slot_a = jnp.where(inner, i - 2, base)
        slot_b = jnp.where(inner, i - 2, base + 1)
        xa = jnp.where(own, x, jnp.where(inner, x - 1, x + 2))
        xb = jnp.where(own, x, jnp.where(inner, x + 1, x + 2))
        xa, ya = place(xa, yh + offset(slot_a))
        xb, yb = place(xb, yh + offset(slot_b))

        @pl.when(i >= 2)
        def _():
            for q in (par, 1 - par):
                arrived(xa, ya, q)

                @pl.when(inner & (q == 0))
                def _():
                    chunk(xa, ya, 0, x_relay.at[slot_a, 0], x_next).start()

                arrived(xb, yb, q)

                @pl.when(inner & (q == 1))
                def _():
                    chunk(xb, yb, 1, x_relay.at[slot_b, 1], x_prev).start()

        queries = qs[...]
        best = top[...]
        for n, (a, b) in enumerate(((xa, ya), (xb, yb))):
            keys = jnp.concatenate([kv[a, b, 0, 0][:SPLIT], kv[a, b, 1, 0]], axis=0)
            found = lax.dot_general(
                keys, queries, (((1,), (1,)), ((), ())), preferred_element_type=jnp.float32
            ) + bias[pl.ds(a, 1), :]
            scores[n] = found
            best = jnp.maximum(best, jnp.max(found, axis=0, keepdims=True))
        scale = jnp.exp(top[...] - best)
        top[...] = best
        row_sum = total[...] * scale
        added = acc[...] * scale
        for n, (a, b) in enumerate(((xa, ya), (xb, yb))):
            weights = jnp.exp(scores[n] - best)
            row_sum = row_sum + jnp.sum(weights, axis=0, keepdims=True)
            values = jnp.concatenate([kv[a, b, 0, 1][:SPLIT], kv[a, b, 1, 1]], axis=0)
            added = added + lax.dot_general(
                values, weights.astype(jnp.bfloat16), (((0,), (0,)), ((), ())), preferred_element_type=jnp.float32
            )
        total[...] = row_sum
        acc[...] = added
        return carry

    lax.fori_loop(0, 8, attend, 0)

    has_any = jnp.max(bias[0:n_x, :], axis=0, keepdims=True) > 0.5 * MASKED_SCORE
    divided = acc[...] / jnp.where(has_any, total[...], 1.0)
    context = jnp.where(has_any, divided, 0.0)
    for h in range(heads):
        out_ref[:, h * HD : (h + 1) * HD] = context[:, h * HD : (h + 1) * HD].T.astype(jnp.bfloat16)

    for copy in [w_far_k, w_far_v, w_own] + fwd + sent:
        copy.wait_send()
    chunk(x, yh, par, z_send, z_pair).wait_send()
    for i in range(2):
        for direction in range(2):
            chunk(x, yh, i, col_y.at[i, direction], yh_next).wait_send()
            for slot in range(4):
                chunk(x, yh, i, col_x.at[slot, i, direction], x_next).wait_send()
        chunk(x, yh, i, y_relay.at[i], yh_next).wait_send()
        for slot in range(4):
            chunk(x, yh, i, x_relay.at[slot, i], x_next).wait_send()


def solution(mesh):
    n_x = n_y = 4
    n_t = mesh.shape["tensor"]

    def on_device(queries, images, kv_weight, q_gain, k_gain, tile_mask):
        tokens, width = queries.shape
        rows, depth = images.shape[1:]
        heads = width // HD
        groups = mesh.shape["dp"]
        any_space = pl.BlockSpec(memory_space=pl.ANY)
        vmem = pl.BlockSpec(memory_space=pltpu.VMEM)
        dma = pltpu.SemaphoreType.DMA
        return pl.pallas_call(
            functools.partial(kernel, (n_x, n_y, n_t, heads)),
            out_shape=jax.ShapeDtypeStruct((tokens, width), jnp.bfloat16),
            in_specs=[any_space, any_space, any_space, vmem, vmem, vmem],
            out_specs=vmem,
            scratch_shapes=[
                pltpu.VMEM((rows, depth), jnp.bfloat16),
                pltpu.VMEM((groups, *kv_weight.shape), jnp.bfloat16),
                pltpu.VMEM((tokens, width), jnp.bfloat16),
                pltpu.VMEM((width, HD), jnp.bfloat16),
                pltpu.VMEM((8, width), jnp.float32),
                pltpu.VMEM((n_t // 2, 2, rows, HD), jnp.bfloat16),
                pltpu.VMEM((n_t // 2, 2, UNIT, HD), jnp.bfloat16),
                pltpu.VMEM((n_t // 2 - 1, 2, UNIT, HD), jnp.bfloat16),
                pltpu.VMEM((n_x, n_y, 2, 2, UNIT, HD), jnp.bfloat16),
                pltpu.VMEM((2, rows, width), jnp.float32),
                pltpu.VMEM((HD, width), jnp.float32),
                pltpu.VMEM((1, width), jnp.float32),
                pltpu.VMEM((1, width), jnp.float32),
                dma((3,)), dma((5,)), dma((5,)),
                dma((n_t // 2, 2)), dma((n_t // 2, 2)),
                dma((n_t // 2 - 1, 2)), dma((n_t // 2 - 1, 2)),
                dma((n_x, n_y, 2)), dma, dma((2,)),
                dma((2, 2)), dma((4, 2, 2)), dma((4, 2)),
            ],
            compiler_params=pltpu.CompilerParams(
                collective_id=0, has_side_effects=True, vmem_limit_bytes=40 * 1024 * 1024
            ),
        )(images, kv_weight, queries, q_gain.reshape(1, HD), k_gain.reshape(1, HD), tile_mask)

    in_specs = (
        P(("section", "dp"), "tensor"),
        P("dp", "section", "tensor"),
        P(None, "tensor", "dp"),
        P(),
        P(),
        P(("section", "dp"), None),
    )
    out_specs = P(("section", "dp"), "tensor")
    return jax.shard_map(on_device, mesh=mesh, in_specs=in_specs, out_specs=out_specs, check_vma=False)
```

time: 190 us -> 80.4 us (0.42)
  waiting for transfers between devices: 94.2 us -> 0 us
  Pallas kernels: 0 us -> 75.2 us
  blocking collectives: 60.9 us -> 0 us
  between operations: 13.7 us -> 0.02 us
  starting transfers between devices: 6.82 us -> 0 us
  matrix products: 4.77 us -> 0 us
  other arithmetic: 2.97 us -> 0 us
    pallas_call x0 -> x1, Pallas kernels: none -> 75.2 us  [on_device(): pl.pallas_call(functools.partial(kernel, (n_x, n_y, n_t, heads)), out_sha...]
    all_gather x1 -> x0, waiting for transfers between devices: 65.9 us -> none  [in_one_piece(): lax.all_gather(both, axis, axis=dim, tiled=True)]
    all_to_all x1 -> x0, blocking collectives: 60.9 us -> none  [summed_on_arrival(): parts = lax.all_to_all(cut_along(shard, dim, size), axis, 0, 0, tiled=True)]
    all_to_all x1 -> x0, waiting for transfers between devices: 25.5 us -> none  [copy_for_each(): lax.all_to_all(jnp.broadcast_to(shard[None], (size, *shard.shape)), axis,...]
    dot_general x5 -> x0, matrix products: 4.77 us -> none  [the longest x1 2.18 us: on_device(): jnp.einsum('thd,nd->htn', q_normed, key_piece, preferred_element_type=jnp...]
    all_to_all x1 -> x0, starting transfers between devices: 3.61 us -> none  [copy_for_each(): lax.all_to_all(jnp.broadcast_to(shard[None], (size, *shard.shape)), axis,...]
    ppermute x1 -> x0, starting transfers between devices: 3.17 us -> none  [partner_2(): lax.ppermute(shard, axis, [(i, i ^ 1 << stride) for i in range(lax.axis_s...]
    unnamed x13 -> x14, local copies, waits for them, and re-layouts: 1.86 us -> 4.88 us
  transfers between devices with their start and end apart: 3 -> 0, of which waited for: 3 -> 0; matrix products, arithmetic and copies ran while one was open for 1% -> 0% of each run, Pallas kernels for 0% -> 0%
where the time goes in v1:
time: 80.4 us; the launch traced here: 80.1 us
  Pallas kernels  75.2 us (94%)
  local copies, waits for them, and re-layouts  4.88 us (6%)
    pallas_call x1, Pallas kernels, on_device(): pl.pallas_call(functools.partial(kernel, (n_x, n_y, n_t, heads)), out_sha...  75.2 us
    unnamed x14, local copies, waits for them, and re-layouts  4.88 us

profile of v1, /device:TPU:6, one launch (start us, length us, event | category | flops | bytes accessed | tf_op | source)
XLA Modules:
  0.0 80.1 jit_solution(16393774538346353259)
XLA Ops:
  0.0 0.0 copy-start.5
  0.0 0.7 copy-done.5
  0.7 0.0 copy-start.3
  0.7 0.0 copy-start.4
  0.7 0.1 copy.7.mask_ref
  0.8 0.5 copy-done.3
  1.3 0.0 copy-done.4
  1.4 0.0 copy-start
  1.4 1.0 %copy-done = bf16[2,512,256]{2,1,0:T(8,128)(2,1)S(1)} copy-done((bf16[2,512,256]{2,1,0:T(8,128)(2,1)S(1)}, bf16[2,512,256]{2,1,0:T(8,128)(2,1)}, u32[]{:S(2)}) %copy-start) | copy-done | bytes 524312
  2.4 0.0 copy-start.1
  2.4 0.9 %copy-done.1 = bf16[1,200,512]{2,1,0:T(8,128)(2,1)S(1)} copy-done((bf16[1,200,512]{2,1,0:T(8,128)(2,1)S(1)}, bf16[1,200,512]{2,1,0:T(8,128)(2,1)}, u32[]{:S(2)}) %copy-start.1) | copy-done | bytes 204824
  3.3 0.0 copy-start.2
  3.3 0.9 %copy-done.2 = bf16[128,512]{1,0:T(8,128)(2,1)S(1)} copy-done((bf16[128,512]{1,0:T(8,128)(2,1)S(1)}, bf16[128,512]{1,0:T(8,128)(2,1)}, u32[]{:S(2)}) %copy-start.2) | copy-done | bytes 131096
  4.2 75.2 %shard_map.64 = bf16[128,512]{1,0:T(8,128)(2,1)S(1)} custom-call(bf16[1,200,512]{2,1,0:T(8,128)(2,1)S(1)} %copy-done.1, bf16[2,512,256]{2,1,0:T(8,128)(2,1)S(1)} %copy-done, bf16[128,512]{1,0:T(8,128)(2,1)S(1)} %copy-done.2, f32[1,128]{1,0:T(1,128)S(1)} %bitcast.2, f32[1,128]{1,0:T(1,128)S(1)} %bitcast.3, s32[128,4]{1,0:T(8,128)S(1)} %copy.7.mask_ref), custom_call_target="tpu_custom_call" | custom-call | tf_op jit(solution)/shard_map/pallas_call | solution.py:287
  79.4 0.7 copy.9
Async XLA Ops:
  0.0 0.7 copy-start.5
  0.7 0.7 copy-start.3
  0.7 0.7 copy-start.4
  1.4 1.0 %copy-start = (bf16[2,512,256]{2,1,0:T(8,128)(2,1)S(1)}, bf16[2,512,256]{2,1,0:T(8,128)(2,1)}, u32[]{:S(2)}) copy-start(bf16[2,512,256]{2,1,0:T(8,128)(2,1)} %w_hbm.1) | copy-start | bytes 1572868
  2.4 0.9 %copy-start.1 = (bf16[1,200,512]{2,1,0:T(8,128)(2,1)S(1)}, bf16[1,200,512]{2,1,0:T(8,128)(2,1)}, u32[]{:S(2)}) copy-start(bf16[1,200,512]{2,1,0:T(8,128)(2,1)} %img_hbm.1) | copy-start | bytes 614404
  3.3 0.9 %copy-start.2 = (bf16[128,512]{1,0:T(8,128)(2,1)S(1)}, bf16[128,512]{1,0:T(8,128)(2,1)}, u32[]{:S(2)}) copy-start(bf16[128,512]{1,0:T(8,128)(2,1)} %q_hbm.1) | copy-start | bytes 393220

commit v2 on v1

--- a/solution.py
+++ b/solution.py
@@ -36,7 +36,7 @@
     partner = {"dp": d + 1 - 2 * core}
     y_next = {"section": section(x, yh + yl), "dp": (1 - yl) * 2 + core}
     y_prev = {"section": section(x, yh + yl - 1), "dp": (1 - yl) * 2 + core}
-    z_next, z_prev = {"tensor": lax.rem(t + 1, n_t)}, {"tensor": lax.rem(t + n_t - 1, n_t)}
+    z_near = tuple({"tensor": lax.rem(t + n_t + step, n_t)} for step in (-2, -1, 1, 2))
     z_pair = {"tensor": t + 1 - 2 * par}
     yh_next, yh_prev = {"section": section(x, yh + 1)}, {"section": section(x, yh - 1)}
     x_next, x_prev = {"section": section(x + 1, yh)}, {"section": section(x - 1, yh)}
@@ -54,7 +54,7 @@
     load_q.start()
 
     barrier = pltpu.get_barrier_semaphore()
-    near = (partner, y_next, y_prev, z_next, z_prev, yh_next, yh_prev, x_next, x_prev)
+    near = (partner, y_next, y_prev, *z_near, yh_next, yh_prev, x_next, x_prev)
     for where in near:
         pl.semaphore_signal(barrier, inc=1, device_id=where, device_id_type=MESH)
     pl.semaphore_wait(barrier, len(near))
@@ -86,14 +86,7 @@
         mean_sq = jnp.mean(rows * rows, axis=-1, keepdims=True)
         normed = rows * lax.rsqrt(mean_sq + EPSILON) * qg_ref[...] * HD ** (-0.5)
         qs[h * HD : (h + 1) * HD, :] = normed.astype(jnp.bfloat16)
-    tokens = mask_ref.shape[0]
-    eye = (
-        lax.broadcasted_iota(jnp.int32, (tokens, tokens), 0) == lax.broadcasted_iota(jnp.int32, (tokens, tokens), 1)
-    ).astype(jnp.float32)
-    seen = lax.dot_general(
-        mask_ref[...].astype(jnp.float32), eye, (((0,), (0,)), ((), ())), preferred_element_type=jnp.float32
-    )
-    hidden = jnp.where(seen > 0.5, 0.0, MASKED_SCORE)
+    hidden = jnp.where(mask_ref[...] > 0, 0.0, MASKED_SCORE)
     for h in range(heads):
         bias[0:n_x, h * HD : (h + 1) * HD] = hidden
     top[...] = jnp.full_like(top, MASKED_SCORE)
@@ -118,41 +111,45 @@
         return part.at[lax.div(u, 2), j, pl.ds(start, UNIT), :]
 
     sent = []
-    for k in range(half_ring):
+    rings = ((1, half_ring, rp, p_send, p_recv), (-1, half_ring - 1, rm, m_send, m_recv))
+
+    def hop(ring, offset, j, src):
+        sign, _, buf, send, recv = rings[ring]
+        jump = 2 - offset % 2
+        where = {"tensor": lax.rem(t + n_t + sign * jump, n_t)}
+        return remote(src, buf.at[offset - 1, j], send.at[offset - 1, j], recv.at[offset - 1, j], where)
+
+    def send_sum(ring, offset, j):
+        sign, longest, buf, send, recv = rings[ring]
+        own = own_part(lax.rem(t + n_t + sign * offset, n_t), j)
+        src = own
+        if offset % 2 == 0 and offset < longest:
+            rows = own[...].astype(jnp.float32)
+            for before in (offset + 1, offset + 2):
+                if before <= longest:
+                    got = buf.at[before - 1, j]
+                    hop(ring, before, j, got).wait_recv()
+                    rows = rows + got[...].astype(jnp.float32)
+            src = buf.at[offset + 1 if offset + 2 <= longest else offset, j]
+            src[...] = rows.astype(jnp.bfloat16)
+        copy = hop(ring, offset, j, src)
+        copy.start()
+        sent.append(copy)
+
+    for offset in range(half_ring, 0, -2):
         for j in range(2):
-            u = lax.rem(t + half_ring - k, n_t)
-            if k == 0:
-                src = own_part(u, j)
-            else:
-                src = rp.at[k - 1, j]
-                remote(src, src, p_send.at[k - 1, j], p_recv.at[k - 1, j], z_next).wait_recv()
-                src[...] = (src[...].astype(jnp.float32) + own_part(u, j)[...].astype(jnp.float32)).astype(jnp.bfloat16)
-            copy = remote(src, rp.at[k, j], p_send.at[k, j], p_recv.at[k, j], z_next)
-            copy.start()
-            sent.append(copy)
-            if k < half_ring - 1:
-                u = lax.rem(t + half_ring + 1 + k, n_t)
-                if k == 0:
-                    src = own_part(u, j)
-                else:
-                    src = rm.at[k - 1, j]
-                    remote(src, src, m_send.at[k - 1, j], m_recv.at[k - 1, j], z_prev).wait_recv()
-                    src[...] = (src[...].astype(jnp.float32) + own_part(u, j)[...].astype(jnp.float32)).astype(
-                        jnp.bfloat16
-                    )
-                copy = remote(src, rm.at[k, j], m_send.at[k, j], m_recv.at[k, j], z_prev)
-                copy.start()
-                sent.append(copy)
+            for ring in range(2):
+                for now in (offset, offset - 1):
+                    if now <= rings[ring][1]:
+                        send_sum(ring, now, j)
 
     for j in range(2):
-        last_p, last_m = rp.at[half_ring - 1, j], rm.at[half_ring - 2, j]
-        remote(last_m, last_m, m_send.at[half_ring - 2, j], m_recv.at[half_ring - 2, j], z_prev).wait_recv()
-        remote(last_p, last_p, p_send.at[half_ring - 1, j], p_recv.at[half_ring - 1, j], z_next).wait_recv()
-        rows = (
-            own_part(t, j)[...].astype(jnp.float32)
-            + last_p[...].astype(jnp.float32)
-            + last_m[...].astype(jnp.float32)
-        )
+        rows = own_part(t, j)[...].astype(jnp.float32)
+        for ring in range(2):
+            for offset in (1, 2):
+                got = rings[ring][2].at[offset - 1, j]
+                hop(ring, offset, j, got).wait_recv()
+                rows = rows + got[...].astype(jnp.float32)
         if j == 0:
             mean_sq = jnp.mean(rows * rows, axis=-1, keepdims=True)
             rows = rows * lax.rsqrt(mean_sq + EPSILON) * kg_ref[...]
@@ -310,9 +307,9 @@
                 dma((2, 2)), dma((4, 2, 2)), dma((4, 2)),
             ],
             compiler_params=pltpu.CompilerParams(
-                collective_id=0, has_side_effects=True, vmem_limit_bytes=40 * 1024 * 1024
+                collective_id=0, has_side_effects=True, vmem_limit_bytes=67043328
             ),
-        )(images, kv_weight, queries, q_gain.reshape(1, HD), k_gain.reshape(1, HD), tile_mask)
+        )(images, kv_weight, queries, q_gain.reshape(1, HD), k_gain.reshape(1, HD), tile_mask.T)
 
     in_specs = (
         P(("section", "dp"), "tensor"),

time: 80.4 us -> 70.9 us (0.88)
  Pallas kernels: 75.2 us -> 68.5 us
  local copies, waits for them, and re-layouts: 4.88 us -> 1.57 us
    pallas_call x1, Pallas kernels: 75.2 us -> 68.5 us  [on_device(): pl.pallas_call(functools.partial(kernel, (n_x, n_y, n_t, heads)), out_sha...]
    unnamed x14 -> x1, local copies, waits for them, and re-layouts: 4.88 us -> 1.57 us
where the time goes in v2:
time: 70.9 us; the launch traced here: 70.1 us
  Pallas kernels  68.5 us (97%)
  local copies, waits for them, and re-layouts  1.57 us (2%)
    pallas_call x1, Pallas kernels, on_device(): pl.pallas_call(functools.partial(kernel, (n_x, n_y, n_t, heads)), out_sha...  68.5 us
    unnamed x1, local copies, waits for them, and re-layouts  1.57 us

profile of v2, /device:TPU:6, one launch (start us, length us, event | category | flops | bytes accessed | tf_op | source)
XLA Modules:
  0.0 70.1 jit_solution(2715648031625195879)
XLA Ops:
  0.0 68.5 %shard_map.64 = bf16[128,512]{1,0:T(8,128)(2,1)} custom-call(bf16[1,200,512]{2,1,0:T(8,128)(2,1)} %img_hbm.1, bf16[2,512,256]{2,1,0:T(8,128)(2,1)} %w_hbm.1, bf16[128,512]{1,0:T(8,128)(2,1)} %q_hbm.1, f32[1,128]{1,0:T(1,128)} %bitcast.4, f32[1,128]{1,0:T(1,128)} %bitcast.5, s32[4,128]{1,0:T(4,128)} %bitcast.3), custom_call_target="tpu_custom_call" | custom-call | tf_op jit(solution)/shard_map/pallas_call | solution.py:284
  68.5 1.6 %copy.8 = bf16[128,512]{1,0:T(8,128)(2,1)} copy(bf16[128,512]{1,0:T(8,128)(2,1)} %shard_map.64) | data formatting | bytes 262144

commit v3 on v2

v3 whole, which is shorter than its diff:
```python
import functools
import math

import jax
import jax.numpy as jnp
from jax import lax
from jax.experimental import pallas as pl
from jax.experimental.pallas import tpu as pltpu
from jax.sharding import PartitionSpec as P

EPSILON = 1e-05
MASKED_SCORE = -1e30
LOGICAL = pl.DeviceIdType.LOGICAL
HD = 128
SPLIT = 96
UNIT = 104
SENDS = 72


def kernel(
    dims,
    img_hbm, w_hbm, q_hbm, qg_hbm, kg_hbm, mask_hbm,
    out_ref,
    img, wbuf, qbuf, qg_ref, kg_ref, mask_ref, qs, bias, part, rp, rm, kv, scores, acc, top, total,
    load_sem, w_send, w_recv, p_send, p_recv, m_send, m_recv, kv_recv, kv_send,
):
    n_x, n_y, n_t, heads, strides = dims
    strides = dict(strides)
    half_ring = n_t // 2
    s, d, t = lax.axis_index("section"), lax.axis_index("dp"), lax.axis_index("tensor")
    x, yh = s // n_y, s % n_y
    yl, core = d // 2, d % 2
    par = t % 2

    def wrap(value, size):
        return jnp.where(value >= size, value - size, value)

    near_x = tuple(wrap(x + step, n_x) for step in range(4))
    near_y = tuple(wrap(yh + step, n_y) for step in range(4))

    def device(a=0, b=0, dp=None, tensor=None):
        section = near_x[a % 4] * n_y + near_y[b % 4]
        dp, tensor = d if dp is None else dp, t if tensor is None else tensor
        return section * strides["section"] + dp * strides["dp"] + tensor * strides["tensor"]

    other, far = d + 1 - 2 * core, (1 - yl) * 2 + core
    across = (1 - yl) * 2 + 1 - core
    low_side = device(dp=far)
    partner = device(dp=other)
    y_next = jnp.where(yl == 0, low_side, device(b=1, dp=far))
    y_prev = jnp.where(yl == 1, low_side, device(b=-1, dp=far))
    z_at = {step: device(tensor=wrap(t + step % n_t, n_t)) for step in (-2, -1, 1, 2)}
    z_pair = device(tensor=t + 1 - 2 * par)
    y_group = tuple(device(b=step) for step in (-1, 1, 2))
    x_group = tuple(device(a=step) for step in (-1, 1, 2))

    def remote(src, dst, send, recv, where):
        return pltpu.make_async_remote_copy(
            src_ref=src, dst_ref=dst, send_sem=send, recv_sem=recv, device_id=where, device_id_type=LOGICAL
        )

    loads = [
        pltpu.make_async_copy(src, dst, load_sem.at[i])
        for i, (src, dst) in enumerate(
            (
                (img_hbm.at[0], img),
                (w_hbm, wbuf.at[d]),
                (q_hbm, qbuf),
                (qg_hbm, qg_ref),
                (mask_hbm, mask_ref),
                (kg_hbm, kg_ref),
            )
        )
    ]
    for load in loads:
        load.start()

    barrier = pltpu.get_barrier_semaphore()
    near = (partner, y_next, y_prev, *z_at.values(), *y_group, *x_group)
    for where in near:
        pl.semaphore_signal(barrier, inc=1, device_id=where, device_id_type=LOGICAL)
    pl.semaphore_wait(barrier, len(near))

    depth = img.shape[1] // 2

    def halves(group, j, stage):
        rows = (pl.ds(0, depth), pl.ds(depth, depth))
        return [(wbuf.at[group, j, rows[i], :], w_send.at[stage, j, i], w_recv.at[stage, j, i]) for i in range(2)]

    sent = []

    def launch(copy):
        copy.start()
        sent.append(copy)

    for j in range(2):
        for i, where in enumerate((y_next, y_prev)):
            dst, send, recv = halves(d, j, 0)[i]
            launch(remote(w_hbm.at[j, pl.ds(i * depth, depth), :], dst, send, recv, where))
        launch(remote(w_hbm.at[j], wbuf.at[d, j], w_send.at[2, j, 0], w_recv.at[2, j, 0], partner))

    loads[0].wait()
    loads[1].wait()
    features = img[...]

    def project(group, j):
        both = jnp.dot(features, wbuf[group, j], preferred_element_type=jnp.float32).astype(jnp.bfloat16)
        part[2 * group, j] = both[:, :HD]
        part[2 * group + 1, j] = both[:, HD:]

    project(d, 0)
    project(d, 1)

    for load in loads[2:]:
        load.wait()
    for h in range(heads):
        rows = qbuf[:, h * HD : (h + 1) * HD].astype(jnp.float32)
        mean_sq = jnp.mean(rows * rows, axis=-1, keepdims=True)
        normed = rows * lax.rsqrt(mean_sq + EPSILON) * qg_ref[...] * HD ** (-0.5)
        qs[h * HD : (h + 1) * HD, :] = normed.astype(jnp.bfloat16)
    hidden = jnp.where(mask_ref[...] > 0, 0.0, MASKED_SCORE)
    for h in range(heads):
        bias[0:n_x, h * HD : (h + 1) * HD] = hidden
    top[...] = jnp.full_like(top, MASKED_SCORE)
    total[...] = jnp.zeros_like(total)
    acc[...] = jnp.zeros_like(acc)

    for j in range(2):
        remote(w_hbm.at[j], wbuf.at[other, j], w_send.at[2, j, 0], w_recv.at[2, j, 0], partner).wait_recv()
        project(other, j)

    def far_weights(j):
        for (dst, send, recv), (_, send_on, recv_on) in zip(halves(far, j, 0), halves(far, j, 1)):
            remote(dst, dst, send, recv, partner).wait_recv()
            launch(remote(dst, dst, send_on, recv_on, partner))
        project(far, j)
        for dst, send, recv in halves(across, j, 1):
            remote(dst, dst, send, recv, partner).wait_recv()
        project(across, j)

    pair, heads_kv = t // 2, n_t // 2

    def own_part(offset, j):
        offset %= n_t
        odd = offset % 2
        start = (1 - par if odd else par) * SPLIT
        head = wrap(pair + offset // 2 + (par if odd else 0), heads_kv)
        return part.at[head, j, pl.ds(pl.multiple_of(start, 16), UNIT), :]

    rings = ((1, half_ring, rp, p_send, p_recv), (-1, half_ring - 1, rm, m_send, m_recv))

    def hop(ring, offset, j, src):
        sign, _, buf, send, recv = rings[ring]
        jump = 2 - offset % 2
        return remote(src, buf.at[offset - 1, j], send.at[offset - 1, j], recv.at[offset - 1, j], z_at[sign * jump])

    def send_sum(ring, offset, j):
        sign, longest, buf, send, recv = rings[ring]
        own = own_part(sign * offset, j)
        src = own
        if offset % 2 == 0 and offset < longest:
            rows = own[...].astype(jnp.float32)
            for before in (offset + 1, offset + 2):
                if before <= longest:
                    got = buf.at[before - 1, j]
                    hop(ring, before, j, got).wait_recv()
                    rows = rows + got[...].astype(jnp.float32)
            src = buf.at[offset + 1 if offset + 2 <= longest else offset, j]
            src[...] = rows.astype(jnp.bfloat16)
        launch(hop(ring, offset, j, src))

    for offset in range(half_ring, 0, -2):
        for j in range(2):
            if offset == half_ring:
                far_weights(j)
            for ring in range(2):
                for now in (offset, offset - 1):
                    if now <= rings[ring][1]:
                        send_sum(ring, now, j)

    def finish(j):
        rows = own_part(0, j)[...].astype(jnp.float32)
        for ring in range(2):
            for offset in (1, 2):
                got = rings[ring][2].at[offset - 1, j]
                hop(ring, offset, j, got).wait_recv()
                rows = rows + got[...].astype(jnp.float32)
        if j == 0:
            mean_sq = jnp.mean(rows * rows, axis=-1, keepdims=True)
            rows = rows * lax.rsqrt(mean_sq + EPSILON) * kg_ref[...]
        kv[x, yh, par, j] = rows.astype(jnp.bfloat16)

    flying = []

    def chunk_at(a, b, q, j, send, where):
        return remote(kv.at[a, b, q, j], kv.at[a, b, q, j], send, kv_recv.at[a, b, q, j], where)

    def chunk(a, b, q, j, send, where):
        return chunk_at(near_x[a % 4], near_y[b % 4], q, j, send, where)

    def arrived(a, b, q, j):
        chunk(a, b, q, j, kv_send.at[0], z_pair).wait_recv()

    def arrived_at(a, b, q, j):
        chunk_at(a, b, q, j, kv_send.at[0], z_pair).wait_recv()

    def forward(a, b, q, j, *where):
        for device in where:
            chunk(a, b, q, j, kv_send.at[len(flying)], device).start()
            flying.append(j)

    both_j = (0, 1)
    opp = 1 - par
    for j in both_j:
        finish(j)
        forward(0, 0, par, j, z_pair, *y_group, *x_group)
    for j in both_j:
        arrived(0, 0, opp, j)
        forward(0, 0, opp, j, *y_group)
    for j in both_j:
        for step in (-1, 1, 2):
            arrived(step, 0, par, j)
            forward(step, 0, par, j, z_pair)
    for slot in (-1, 1, 2):
        for j in both_j:
            arrived(0, slot, par, j)
            forward(0, slot, par, j, *x_group)

    def events_at(i):
        @pl.when(i == 2)
        def _():
            for j in both_j:
                for step in (-1, 1, 2):
                    arrived(step, -1, par, j)
                    forward(step, -1, par, j, z_pair)
            for slot in (1, 2):
                for j in both_j:
                    arrived(0, slot, opp, j)
                    forward(0, slot, opp, j, *x_group)
            for j in both_j:
                for step in (-1, 1, 2):
                    arrived(step, 1, par, j)

    def pick(near, n):
        return jnp.where(n == 0, near[0], jnp.where(n == 1, near[3], jnp.where(n == 2, near[1], near[2])))

    def attend(i, carry):
        events_at(i)
        slot, half = i // 2, i % 2
        xa, xb = pick(near_x, 2 * half), pick(near_x, 2 * half + 1)
        ya = yb = pick(near_y, slot)

        @pl.when((slot < 3) & (i > 0) & (i != 4))
        def _():
            for j in both_j:
                arrived_at(xa, ya, opp, j)

        @pl.when(i == 7)
        def _():
            for j in both_j:
                arrived_at(xa, ya, par, j)
                arrived_at(xa, ya, opp, j)

        for j in both_j:
            arrived_at(xb, yb, opp, j)

        @pl.when(slot == 3)
        def _():
            for j in both_j:
                arrived_at(xb, yb, par, j)

        queries = qs[...]
        best = top[...]
        for n, (a, b) in enumerate(((xa, ya), (xb, yb))):
            keys = jnp.concatenate([kv[a, b, 0, 0][:SPLIT], kv[a, b, 1, 0]], axis=0)
            found = lax.dot_general(
                keys, queries, (((1,), (1,)), ((), ())), preferred_element_type=jnp.float32
            )
            scores[n] = found
            best = jnp.maximum(best, jnp.max(found, axis=0, keepdims=True) + bias[pl.ds(a, 1), :])
        scale = jnp.exp(top[...] - best)
        top[...] = best
        row_sum = total[...] * scale
        added = acc[...] * scale
        for n, (a, b) in enumerate(((xa, ya), (xb, yb))):
            weights = jnp.exp(scores[n] + jnp.where(bias[pl.ds(a, 1), :] < 0, MASKED_SCORE, -best))
            row_sum = row_sum + jnp.sum(weights, axis=0, keepdims=True)
            values = jnp.concatenate([kv[a, b, 0, 1][:SPLIT], kv[a, b, 1, 1]], axis=0)
            added = added + lax.dot_general(
                values, weights.astype(jnp.bfloat16), (((0,), (0,)), ((), ())), preferred_element_type=jnp.float32
            )
        total[...] = row_sum
        acc[...] = added
        return carry

    lax.fori_loop(0, 8, attend, 0)

    has_any = jnp.max(bias[0:n_x, :], axis=0, keepdims=True) > 0.5 * MASKED_SCORE
    divided = acc[...] / jnp.where(has_any, total[...], 1.0)
    context = jnp.where(has_any, divided, 0.0)
    for h in range(heads):
        out_ref[:, h * HD : (h + 1) * HD] = context[:, h * HD : (h + 1) * HD].T.astype(jnp.bfloat16)

    for copy in sent:
        copy.wait_send()
    for i, j in enumerate(flying):
        chunk(0, 0, 0, j, kv_send.at[i], z_pair).wait_send()


def solution(mesh):
    n_x = n_y = 4
    n_t = mesh.shape["tensor"]
    names = mesh.axis_names
    strides = tuple((name, math.prod(mesh.shape[m] for m in names[i + 1 :])) for i, name in enumerate(names))

    def on_device(queries, images, kv_weight, q_gain, k_gain, tile_mask):
        tokens, width = queries.shape
        rows, depth = images.shape[1:]
        heads = width // HD
        groups = mesh.shape["dp"]
        any_space = pl.BlockSpec(memory_space=pltpu.HBM)
        vmem = pl.BlockSpec(memory_space=pltpu.VMEM)
        dma = pltpu.SemaphoreType.DMA
        return pl.pallas_call(
            functools.partial(kernel, (n_x, n_y, n_t, heads, strides)),
            out_shape=jax.ShapeDtypeStruct((tokens, width), jnp.bfloat16),
            in_specs=[any_space] * 6,
            out_specs=vmem,
            scratch_shapes=[
                pltpu.VMEM((rows, depth), jnp.bfloat16),
                pltpu.VMEM((groups, *kv_weight.shape), jnp.bfloat16),
                pltpu.VMEM((tokens, width), jnp.bfloat16),
                pltpu.VMEM((1, HD), jnp.float32),
                pltpu.VMEM((1, HD), jnp.float32),
                pltpu.VMEM((n_x, tokens), jnp.int32),
                pltpu.VMEM((width, HD), jnp.bfloat16),
                pltpu.VMEM((8, width), jnp.float32),
                pltpu.VMEM((n_t // 2, 2, rows, HD), jnp.bfloat16),
                pltpu.VMEM((n_t // 2, 2, UNIT, HD), jnp.bfloat16),
                pltpu.VMEM((n_t // 2 - 1, 2, UNIT, HD), jnp.bfloat16),
                pltpu.VMEM((n_x, n_y, 2, 2, UNIT, HD), jnp.bfloat16),
                pltpu.VMEM((2, rows, width), jnp.float32),
                pltpu.VMEM((HD, width), jnp.float32),
                pltpu.VMEM((1, width), jnp.float32),
                pltpu.VMEM((1, width), jnp.float32),
                dma((6,)), dma((3, 2, 2)), dma((3, 2, 2)),
                dma((n_t // 2, 2)), dma((n_t // 2, 2)),
                dma((n_t // 2 - 1, 2)), dma((n_t // 2 - 1, 2)),
                dma((n_x, n_y, 2, 2)), dma((SENDS,)),
            ],
            compiler_params=pltpu.CompilerParams(
                collective_id=0, has_side_effects=True, vmem_limit_bytes=67043328
            ),
        )(images, kv_weight, queries, q_gain.reshape(1, HD), k_gain.reshape(1, HD), tile_mask.T)

    in_specs = (
        P(("section", "dp"), "tensor"),
        P("dp", "section", "tensor"),
        P(None, "tensor", "dp"),
        P(),
        P(),
        P(("section", "dp"), None),
    )
    out_specs = P(("section", "dp"), "tensor")
    return jax.shard_map(on_device, mesh=mesh, in_specs=in_specs, out_specs=out_specs, check_vma=False)
```

time: 70.9 us -> 70.1 us (0.989)
  the two profiles are of different devices: /device:TPU:6 before, /device:TPU:8 now
where the time goes in v3:
time: 70.1 us; the launch traced here: 70 us
  Pallas kernels  68.4 us (98%)
  local copies, waits for them, and re-layouts  1.57 us (2%)
    pallas_call x1, Pallas kernels, on_device(): pl.pallas_call(functools.partial(kernel, (n_x, n_y, n_t, heads, strides))...  68.4 us
    unnamed x1, local copies, waits for them, and re-layouts  1.57 us

profile of v3, /device:TPU:8, one launch (start us, length us, event | category | flops | bytes accessed | tf_op | source)
XLA Modules:
  0.0 70.0 jit_solution(13535191499434074433)
XLA Ops:
  0.0 68.4 %shard_map.64 = bf16[128,512]{1,0:T(8,128)(2,1)} custom-call(bf16[1,200,512]{2,1,0:T(8,128)(2,1)} %img_hbm.1, bf16[2,512,256]{2,1,0:T(8,128)(2,1)} %w_hbm.1, bf16[128,512]{1,0:T(8,128)(2,1)} %q_hbm.1, f32[1,128]{1,0:T(1,128)} %bitcast.4, f32[1,128]{1,0:T(1,128)} %bitcast.5, s32[4,128]{1,0:T(4,128)} %bitcast.3), custom_call_target="tpu_custom_call" | custom-call | tf_op jit(solution)/shard_map/pallas_call | solution.py:324
  68.4 1.6 %copy.8 = bf16[128,512]{1,0:T(8,128)(2,1)} copy(bf16[128,512]{1,0:T(8,128)(2,1)} %shard_map.64) | data formatting | bytes 262144

commit v4 on v3

--- a/solution.py
+++ b/solution.py
@@ -216,15 +216,14 @@
         forward(0, 0, par, j, z_pair, *y_group, *x_group)
     for j in both_j:
         arrived(0, 0, opp, j)
-        forward(0, 0, opp, j, *y_group)
+        forward(0, 0, opp, j, *y_group[:2], *x_group)
     for j in both_j:
         for step in (-1, 1, 2):
             arrived(step, 0, par, j)
-            forward(step, 0, par, j, z_pair)
     for slot in (-1, 1, 2):
         for j in both_j:
             arrived(0, slot, par, j)
-            forward(0, slot, par, j, *x_group)
+            forward(0, slot, par, j, *((z_pair, *x_group) if slot == 2 else x_group))
 
     def events_at(i):
         @pl.when(i == 2)
@@ -236,10 +235,12 @@
             for slot in (1, 2):
                 for j in both_j:
                     arrived(0, slot, opp, j)
-                    forward(0, slot, opp, j, *x_group)
+                    if slot == 2:
+                        forward(0, slot, opp, j, *x_group)
             for j in both_j:
                 for step in (-1, 1, 2):
                     arrived(step, 1, par, j)
+                    forward(step, 1, par, j, z_pair)
 
     def pick(near, n):
         return jnp.where(n == 0, near[0], jnp.where(n == 1, near[3], jnp.where(n == 2, near[1], near[2])))

time: 70.1 us -> 69.3 us (0.989)
  Pallas kernels: 68.4 us -> 67.6 us
    pallas_call x1, Pallas kernels: 68.4 us -> 67.6 us  [on_device(): pl.pallas_call(functools.partial(kernel, (n_x, n_y, n_t, heads, strides))...]
where the time goes in v4:
time: 69.3 us; the launch traced here: 69.2 us
  Pallas kernels  67.6 us (98%)
  local copies, waits for them, and re-layouts  1.57 us (2%)
    pallas_call x1, Pallas kernels, on_device(): pl.pallas_call(functools.partial(kernel, (n_x, n_y, n_t, heads, strides))...  67.6 us
    unnamed x1, local copies, waits for them, and re-layouts  1.57 us

profile of v4, /device:TPU:8, one launch (start us, length us, event | category | flops | bytes accessed | tf_op | source)
XLA Modules:
  0.0 69.2 jit_solution(161965175360613969)
XLA Ops:
  0.0 67.6 %shard_map.64 = bf16[128,512]{1,0:T(8,128)(2,1)} custom-call(bf16[1,200,512]{2,1,0:T(8,128)(2,1)} %img_hbm.1, bf16[2,512,256]{2,1,0:T(8,128)(2,1)} %w_hbm.1, bf16[128,512]{1,0:T(8,128)(2,1)} %q_hbm.1, f32[1,128]{1,0:T(1,128)} %bitcast.4, f32[1,128]{1,0:T(1,128)} %bitcast.5, s32[4,128]{1,0:T(4,128)} %bitcast.3), custom_call_target="tpu_custom_call" | custom-call | tf_op jit(solution)/shard_map/pallas_call | solution.py:325
  67.6 1.6 %copy.8 = bf16[128,512]{1,0:T(8,128)(2,1)} copy(bf16[128,512]{1,0:T(8,128)(2,1)} %shard_map.64) | data formatting | bytes 262144

commit v5 on v4

--- a/solution.py
+++ b/solution.py
@@ -226,21 +226,21 @@
             forward(0, slot, par, j, *((z_pair, *x_group) if slot == 2 else x_group))
 
     def events_at(i):
+        @pl.when(i == 1)
+        def _():
+            for slot in (-1, 1):
+                for j in both_j:
+                    for step in (-1, 1, 2):
+                        arrived(step, slot, par, j)
+                        forward(step, slot, par, j, z_pair)
+
         @pl.when(i == 2)
         def _():
-            for j in both_j:
-                for step in (-1, 1, 2):
-                    arrived(step, -1, par, j)
-                    forward(step, -1, par, j, z_pair)
             for slot in (1, 2):
                 for j in both_j:
                     arrived(0, slot, opp, j)
                     if slot == 2:
                         forward(0, slot, opp, j, *x_group)
-            for j in both_j:
-                for step in (-1, 1, 2):
-                    arrived(step, 1, par, j)
-                    forward(step, 1, par, j, z_pair)
 
     def pick(near, n):
         return jnp.where(n == 0, near[0], jnp.where(n == 1, near[3], jnp.where(n == 2, near[1], near[2])))

time: 69.3 us -> 68.9 us (level)
  the two profiles are of different devices: /device:TPU:8 before, /device:TPU:6 now
where the time goes in v5:
time: 68.9 us; the launch traced here: 67.6 us
  Pallas kernels  66.1 us (96%)
  local copies, waits for them, and re-layouts  1.57 us (2%)
    pallas_call x1, Pallas kernels, on_device(): pl.pallas_call(functools.partial(kernel, (n_x, n_y, n_t, heads, strides))...  66.1 us
    unnamed x1, local copies, waits for them, and re-layouts  1.57 us

profile of v5, /device:TPU:6, one launch (start us, length us, event | category | flops | bytes accessed | tf_op | source)
XLA Modules:
  0.0 67.6 jit_solution(1705753883641509874)
XLA Ops:
  0.0 66.1 %shard_map.64 = bf16[128,512]{1,0:T(8,128)(2,1)} custom-call(bf16[1,200,512]{2,1,0:T(8,128)(2,1)} %img_hbm.1, bf16[2,512,256]{2,1,0:T(8,128)(2,1)} %w_hbm.1, bf16[128,512]{1,0:T(8,128)(2,1)} %q_hbm.1, f32[1,128]{1,0:T(1,128)} %bitcast.4, f32[1,128]{1,0:T(1,128)} %bitcast.5, s32[4,128]{1,0:T(4,128)} %bitcast.3), custom_call_target="tpu_custom_call" | custom-call | tf_op jit(solution)/shard_map/pallas_call | solution.py:325
  66.1 1.6 %copy.8 = bf16[128,512]{1,0:T(8,128)(2,1)} copy(bf16[128,512]{1,0:T(8,128)(2,1)} %shard_map.64) | data formatting | bytes 262144
